TPU v7x, 512 devices: a whole 4x8x8 slice. The times are simulated.
512 devices in a mesh: dp: 16 (over y_lo, z), gx: 8 (over x, core), gy: 4 (over y_hi).
Axes of the slice: x: 4, y: 8 (y_hi: 4, y_lo: 2; y = y_hi * 2 + y_lo), z: 8, core: 2. Of those that a mesh axis runs over, the one named last changes fastest.
Arguments:
- fields: bfloat16 [16, 20, 32, 16384], P('dp', None, None, ('gx', 'gy')), may hold values from -6 to 6
- cotangent: bfloat16 [16, 20, 32, 16384], P('dp', None, None, ('gx', 'gy')), may hold values from -6 to 6
- mix_weight: bfloat16 [20, 20], replicated, may hold values from -1.25 to 1.25
- spectral_weight: bfloat16 [288, 2, 20, 20], P(('gx', 'gy')), may hold values from -1 to 1
Outputs:
- output: bfloat16 [16, 20, 32, 16384], P('dp', None, None, ('gx', 'gy'))
- spectral_grad: float32 [288, 2, 20, 20], P(('gx', 'gy'))
- mixing_grad: float32 [20, 20], replicated
All inputs are finite; a program needn't handle non-finite values.
Results may differ from a plain program's by a relative error of at most 0.0031.
Values may be sent and summed in bfloat16 or wider, within the bound.
A program may use at most 64 MiB of HBM per device.

v0:
```python
import math
import jax
import jax.numpy as jnp
from jax import lax
from jax.sharding import PartitionSpec as P

NX = 128
NY = 128
KX = 24
KY = 12
P_SIZE = 32
MODES = 288
HI = lax.Precision.HIGHEST


def gelu_value(h):
    k = math.sqrt(2.0 / math.pi)
    t = jnp.tanh(k * (h + 0.044715 * h * h * h))
    return 0.5 * h * (1.0 + t)


def gelu_slope(h):
    k = math.sqrt(2.0 / math.pi)
    t = jnp.tanh(k * (h + 0.044715 * h * h * h))
    return 0.5 * (1.0 + t) + 0.5 * h * (1.0 - t * t) * k * (1.0 + 3.0 * 0.044715 * h * h)


def axis_table(waves, n):
    cells = jnp.arange(n, dtype=jnp.int32)
    angle = 2.0 * math.pi / n * (waves[:, None] * cells[None, :] % n).astype(jnp.float32)
    return (jnp.cos(angle), jnp.sin(angle))


def tables():
    index = jnp.arange(KX, dtype=jnp.int32)
    waves_x = jnp.where(index < KX // 2, index, NX - KX + index)
    cos_x, sin_x = axis_table(waves_x, NX)
    cos_y, sin_y = axis_table(jnp.arange(KY, dtype=jnp.int32), NY)
    return (cos_x, sin_x, cos_y, sin_y)


def forward_dft(data, scale):
    cos_x, sin_x, cos_y, sin_y = tables()
    a_re = jnp.einsum("cpxy,ky->cpxk", data, cos_y, precision=HI)
    a_im = -jnp.einsum("cpxy,ky->cpxk", data, sin_y, precision=HI)
    s_re = jnp.einsum("cpxk,jx->jkcp", a_re, cos_x, precision=HI) + jnp.einsum(
        "cpxk,jx->jkcp", a_im, sin_x, precision=HI
    )
    s_im = jnp.einsum("cpxk,jx->jkcp", a_im, cos_x, precision=HI) - jnp.einsum(
        "cpxk,jx->jkcp", a_re, sin_x, precision=HI
    )
    chans, planes = (data.shape[0], data.shape[1])
    return scale * jnp.stack(
        [s_re.reshape(MODES, chans, planes), s_im.reshape(MODES, chans, planes)], axis=1
    )


def inverse_dft(vals, scale):
    cos_x, sin_x, cos_y, sin_y = tables()
    chans, planes = (vals.shape[2], vals.shape[3])
    v_re = vals[:, 0].reshape(KX, KY, chans, planes)
    v_im = vals[:, 1].reshape(KX, KY, chans, planes)
    b_re = jnp.einsum("jkdp,jx->dpxk", v_re, cos_x, precision=HI) - jnp.einsum(
        "jkdp,jx->dpxk", v_im, sin_x, precision=HI
    )
    b_im = jnp.einsum("jkdp,jx->dpxk", v_re, sin_x, precision=HI) + jnp.einsum(
        "jkdp,jx->dpxk", v_im, cos_x, precision=HI
    )
    return scale * (
        jnp.einsum("dpxk,ky->dpxy", b_re, cos_y, precision=HI)
        - jnp.einsum("dpxk,ky->dpxy", b_im, sin_y, precision=HI)
    )


def spectral_mix(spec, weight):
    w = weight.astype(jnp.float32)
    v_re = jnp.einsum("mcp,mcd->mdp", spec[:, 0], w[:, 0], precision=HI) - jnp.einsum(
        "mcp,mcd->mdp", spec[:, 1], w[:, 1], precision=HI
    )
    v_im = jnp.einsum("mcp,mcd->mdp", spec[:, 0], w[:, 1], precision=HI) + jnp.einsum(
        "mcp,mcd->mdp", spec[:, 1], w[:, 0], precision=HI
    )
    return jnp.stack([v_re, v_im], axis=1)


def grads_of(spec, gspec):
    g_re = jnp.einsum("mcp,mdp->mcd", spec[:, 0], gspec[:, 0], precision=HI) + jnp.einsum(
        "mcp,mdp->mcd", spec[:, 1], gspec[:, 1], precision=HI
    )
    g_im = jnp.einsum("mcp,mdp->mcd", spec[:, 0], gspec[:, 1], precision=HI) - jnp.einsum(
        "mcp,mdp->mcd", spec[:, 1], gspec[:, 0], precision=HI
    )
    return jnp.stack([g_re, g_im], axis=1)


def to_planes(block):
    chans, planes, rows_x, full_y = block.shape
    size_x = lax.axis_size("gx")
    size_y = lax.axis_size("gy")
    moved = lax.all_to_all(
        lax.all_to_all(block, "gx", split_axis=1, concat_axis=2, tiled=True),
        "gy",
        split_axis=1,
        concat_axis=2,
        tiled=True,
    )
    own = moved.shape[1]
    moved = moved.reshape(chans, own, size_y, size_x, rows_x, full_y)
    moved = jnp.transpose(moved, (0, 1, 3, 2, 4, 5))
    return moved.reshape(chans, own, size_x * size_y * rows_x, full_y)


def to_cells(plane_block):
    chans, own, full_x, full_y = plane_block.shape
    size_x = lax.axis_size("gx")
    size_y = lax.axis_size("gy")
    rows_x = full_x // (size_x * size_y)
    moved = lax.all_to_all(
        lax.all_to_all(plane_block, "gx", split_axis=2, concat_axis=1, tiled=True),
        "gy",
        split_axis=2,
        concat_axis=1,
        tiled=True,
    )
    moved = moved.reshape(chans, size_y, size_x, own, rows_x, full_y)
    moved = jnp.transpose(moved, (0, 2, 1, 3, 4, 5))
    return moved.reshape(chans, size_x * size_y * own, rows_x, full_y)


def local(fields, cotangent, mix_weight, spectral_weight):
    flat = fields[0]
    grad_out = cotangent[0].astype(jnp.float32)
    chans, planes, cells = flat.shape
    rows_x = cells // NY
    norm_in = 1.0 / math.sqrt(NX * NY)
    norm_out = 1.0 / math.sqrt(MODES)
    samples = lax.axis_size("dp")
    mixed = jnp.einsum("cpq,cd->dpq", flat, mix_weight, preferred_element_type=jnp.float32)
    plane_field = to_planes(flat.reshape(chans, planes, rows_x, NY)).astype(jnp.float32)
    spec = forward_dft(plane_field, norm_in)
    full_weight = lax.all_gather(spectral_weight, ("gx", "gy"), axis=0, tiled=True)
    vals = spectral_mix(spec, full_weight)
    branch = to_cells(inverse_dft(vals, norm_out)).reshape(chans, planes, cells)
    pre = branch + mixed
    output = gelu_value(pre).astype(jnp.bfloat16).reshape(1, chans, planes, cells)
    back = (grad_out * gelu_slope(pre)).astype(jnp.bfloat16)
    local_mix = jnp.einsum("cpq,dpq->cd", flat, back, preferred_element_type=jnp.float32)
    mix_scale = 1.0 / math.sqrt(samples * P_SIZE * NX * NY)
    spec_scale = 1.0 / math.sqrt(samples * P_SIZE)
    plane_back = to_planes(back.reshape(chans, planes, rows_x, NY)).astype(jnp.float32)
    gspec = forward_dft(plane_back, norm_out)
    local_spec = grads_of(spec, gspec)
    share = lax.psum_scatter(local_spec, ("gx", "gy"), scatter_dimension=0, tiled=True)
    spectral_grad = lax.psum(share, "dp") * spec_scale
    mixing_grad = lax.psum(local_mix, ("dp", "gx", "gy")) * mix_scale
    return (output, spectral_grad, mixing_grad)


def solution(mesh):
    return jax.shard_map(
        local,
        mesh=mesh,
        in_specs=(
            P("dp", None, None, ("gx", "gy")),
            P("dp", None, None, ("gx", "gy")),
            P(),
            P(("gx", "gy"), None, None, None),
        ),
        out_specs=(P("dp", None, None, ("gx", "gy")), P(("gx", "gy"), None, None, None), P()),
        check_vma=False,
    )
```

profile of v0, /device:TPU:2, one launch (start us, length us, event | category | flops | bytes accessed | tf_op | source)
XLA Modules:
  0.0 713.6 jit_solution(4944024013968660867)
XLA Ops:
  7.2 1.6 reshape_squeeze.3
  8.8 1.1 copy.251
  9.9 10.0 %all-to-all-start = ((bf16[20,32,4,128]{3,2,0,1:T(4,128)(2,1)}), bf16[20,32,4,128]{3,2,0,1:T(4,128)(2,1)}, u32[]{:S(2)}, u32[]{:S(2)}) async-start(bf16[20,32,4,128]{3,2,0,1:T(4,128)(2,1)} %copy.251), calls=%async_computation | async-start | bytes 1310720 | tf_op jit(solution)/shard_map/all_to_all | solution.py:101
  19.9 112.9 %all_gather.3 = bf16[288,2,20,20]{3,1,2,0:T(2,128)(2,1)S(1)} all-gather(bf16[9,2,20,20]{3,1,2,0:T(2,128)(2,1)S(1)} %copy-done.5), channel_id=1, replica_groups=mesh['dp'=16,'gx'=8,'gy'=4] {'gx','gy'}, dimensions={0}, use_global_device_ids=true | all-gather | bytes 475200 | tf_op jit(solution)/shard_map/all_gather | solution.py:141
  132.7 1.3 copy.252
  134.0 0.3 copy.253
  134.4 0.9 copy.254
  135.2 4.8 all-to-all-start.1
  140.1 5.6 fusion.165
  145.7 6.4 copy.317
  152.1 4.7 copy.318
  156.8 1.9 all-to-all-done.1
  158.7 1.2 copy.255
  159.8 0.3 copy.256
  160.1 0.6 fusion.9
  160.8 0.6 convolution_bitcast_fusion
  161.4 0.9 fusion.33
  162.3 0.9 fusion.29
  163.3 0.9 fusion.15
  164.2 0.9 fusion.14
  165.1 0.3 copy.262
  165.4 0.2 stack.24
  165.6 0.3 copy.259
  166.2 0.3 fusion.22
  166.7 0.2 copy.265
  166.9 0.4 fusion.41
  167.3 0.4 fusion.49
  167.9 0.2 copy.266
  168.1 0.4 fusion.12
  168.5 0.4 fusion.13
  168.9 2.2 fusion.24
  171.1 2.2 fusion.8
  173.3 1.3 copy.271
  174.7 20.8 %all_to_all.81 = f32[20,1,128,128]{3,1,0,2:T(1,128)S(1)} all-to-all(f32[20,1,128,128]{3,1,0,2:T(1,128)S(1)} %copy.271), channel_id=1, replica_groups=mesh['dp'=16,'gx'=8,'gy'=4] {'gx'}, dimensions={2} | all-to-all | bytes 2621440 | tf_op jit(solution)/shard_map/all_to_all | solution.py:119
  195.7 0.4 copy.273
  196.1 39.4 %all_to_all.82 = f32[20,8,16,128]{3,1,0,2:T(8,128)S(1)} all-to-all(f32[20,8,16,128]{3,1,0,2:T(8,128)S(1)} %copy.273), channel_id=1, replica_groups=mesh['dp'=16,'gx'=8,'gy'=4] {'gy'}, dimensions={2} | all-to-all | bytes 2621440 | tf_op jit(solution)/shard_map/all_to_all | solution.py:118
  235.4 0.8 copy.357
  236.3 0.5 reshape_reshape.3
  236.8 0.5 copy-done.4
  237.4 4.7 fusion.6
  242.1 0.3 reshape.261
  242.4 14.0 %all_to_all.83 = bf16[20,32,4,128]{3,2,0,1:T(4,128)(2,1)S(1)} all-to-all(bf16[20,32,4,128]{3,2,0,1:T(4,128)(2,1)S(1)} %reshape.261), channel_id=1, replica_groups=mesh['dp'=16,'gx'=8,'gy'=4] {'gx'}, dimensions={1} | all-to-all | bytes 1310720 | tf_op jit(solution)/shard_map/all_to_all | solution.py:101
  256.4 0.3 copy.281
  256.8 22.2 %all_to_all.84 = bf16[20,4,32,128]{3,2,0,1:T(8,128)(2,1)S(1)} all-to-all(bf16[20,4,32,128]{3,2,0,1:T(8,128)(2,1)S(1)} %copy.282), channel_id=1, replica_groups=mesh['dp'=16,'gx'=8,'gy'=4] {'gy'}, dimensions={1} | all-to-all | bytes 1310720 | tf_op jit(solution)/shard_map/all_to_all | solution.py:100
  279.1 0.3 copy.284
  279.3 0.6 fusion.59
  280.0 0.6 fusion.63
  280.6 0.9 fusion.27
  281.6 0.9 fusion.35
  282.5 0.9 fusion.11
  283.4 0.9 fusion.10
  284.4 0.3 copy.289
  284.6 0.2 stack.27
  284.8 0.3 copy.287
  285.7 6.0 copy.290
  291.8 1.3 dynamic-slice
  293.8 1.0 copy.292
  294.8 0.7 convolution_bitcast_fusion.1
  295.5 107.2 %psum.15 = f32[20,20]{0,1:T(8,128)S(1)} all-reduce(f32[20,20]{0,1:T(8,128)S(1)} %convolution_bitcast_fusion.1), channel_id=1, replica_groups=mesh['dp'=16,'gx'=8,'gy'=4] {'dp','gx','gy'}, use_global_device_ids=true, to_apply=%region_2.3 | all-reduce | flops 400 | bytes 3200 | tf_op jit(solution)/shard_map/psum | solution.py:155
  402.7 0.7 copy.293
  403.4 233.1 %all-reduce.3.cloned.1.call-done = f32[288,2,20,20]{3,1,2,0:T(2,128)} async-done(((f32[288,2,20,20]{3,1,2,0:T(2,128)}), f32[288,2,20,20]{3,1,2,0:T(2,128)}) %all-reduce.3.cloned.1.call-update) | async-done | bytes 921616
  636.4 0.9 constant_dynamic-slice_fusion
  637.4 68.6 %psum.14 = f32[9,2,20,20]{3,1,2,0:T(2,128)S(1)} all-reduce(f32[9,2,20,20]{3,1,2,0:T(2,128)S(1)} %constant_dynamic-slice_fusion), channel_id=1, replica_groups=mesh['dp'=16,'gx'=8,'gy'=4] {'dp'}, use_global_device_ids=true, to_apply=%region_1.2 | all-reduce | flops 7200 | bytes 57600 | tf_op jit(solution)/shard_map/psum | solution.py:154
  706.0 0.8 broadcast_multiply_fusion
  (34 shorter events, 1.5 us)
Async XLA Ops:
  7.2 229.7 %copy-start = (bf16[20,20]{1,0:T(8,128)(2,1)S(1)}, bf16[20,20]{1,0:T(8,128)(2,1)}, u32[]{:S(2)}) copy-start(bf16[20,20]{1,0:T(8,128)(2,1)} %param.6) | copy-start | bytes 2404
  8.8 11.0 %copy-start.5 = (bf16[9,2,20,20]{3,1,2,0:T(2,128)(2,1)S(1)}, bf16[9,2,20,20]{3,1,2,0:T(2,128)(2,1)}, u32[]{:S(2)}) copy-start(bf16[9,2,20,20]{3,1,2,0:T(2,128)(2,1)} %param.7) | copy-start | bytes 43204
  9.9 122.8 %all-to-all-start = ((bf16[20,32,4,128]{3,2,0,1:T(4,128)(2,1)}), bf16[20,32,4,128]{3,2,0,1:T(4,128)(2,1)}, u32[]{:S(2)}, u32[]{:S(2)}) async-start(bf16[20,32,4,128]{3,2,0,1:T(4,128)(2,1)} %copy.251), calls=%async_computation | async-start | bytes 1310720 | tf_op jit(solution)/shard_map/all_to_all | solution.py:101
  135.2 23.4 %all-to-all-start.1 = ((bf16[20,4,32,128]{3,2,0,1:T(8,128)(2,1)}), bf16[20,4,32,128]{3,2,0,1:T(8,128)(2,1)}, u32[]{:S(2)}, u32[]{:S(2)}) async-start(bf16[20,4,32,128]{3,2,0,1:T(8,128)(2,1)} %copy.254), calls=%async_computation.1 | async-start | bytes 1310720 | tf_op jit(solution)/shard_map/all_to_all | solution.py:100
  140.1 496.3 %all-reduce.3.cloned.1.call-start = ((), (), s32[]{:S(2)}) async-start(), calls=%async_computation.6 | async-start | bytes 11796480
  145.7 6.4 copy-start.1
  161.4 4.8 copy-start.2
  236.3 1.1 copy-start.4
  291.8 2.0 copy-start.3
Sparse Core Ops, SparseCore 0:
  291.9 344.4 all-reduce.2
where the time goes:
time: 714 us
  blocking collectives  385 us (54%)
  waiting for transfers between devices  235 us (33%)
  local copies, waits for them, and re-layouts  40.8 us (6%)
  matrix products  21.4 us (3%)
  between operations  15.1 us (2%)
  starting transfers between devices  14.8 us (2%)
    unnamed x2, waiting for transfers between devices  233 us
    all_gather x1, blocking collectives, local(): lax.all_gather(spectral_weight, ('gx', 'gy'), axis=0, tiled=True)  113 us
    psum x1, blocking collectives, local(): mixing_grad = lax.psum(local_mix, ('dp', 'gx', 'gy')) * mix_scale  107 us
    psum x1, blocking collectives, local(): spectral_grad = lax.psum(share, 'dp') * spec_scale  68.6 us
    all_to_all x1, blocking collectives, to_cells(): lax.all_to_all(lax.all_to_all(plane_block, 'gx', split_axis=2, concat_axi...  39.4 us
    all_to_all x1, blocking collectives, to_planes(): lax.all_to_all(lax.all_to_all(block, 'gx', split_axis=1, concat_axis=2, t...  22.2 us
    all_to_all x1, blocking collectives, to_cells(): lax.all_to_all(plane_block, 'gx', split_axis=2, concat_axis=1, tiled=True)  20.8 us
    unnamed x21, local copies, waits for them, and re-layouts  15.6 us
  transfers between devices with their start and end apart: 3, of which 2 were waited for; matrix products, arithmetic and copies ran while one was open for 3% of the time, Pallas kernels for 0%

commit v1 on v0

--- a/solution.py
+++ b/solution.py
@@ -152,7 +152,7 @@
     local_spec = grads_of(spec, gspec)
     share = lax.psum_scatter(local_spec, ("gx", "gy"), scatter_dimension=0, tiled=True)
     spectral_grad = lax.psum(share, "dp") * spec_scale
-    mixing_grad = lax.psum(local_mix, ("dp", "gx", "gy")) * mix_scale
+    mixing_grad = lax.psum(lax.psum(local_mix, "dp"), ("gx", "gy")) * mix_scale
     return (output, spectral_grad, mixing_grad)
 
 

time: 714 us -> 856 us (1.20)
  the two profiles are of different devices: /device:TPU:2 before, /device:TPU:8 now
where the time goes in v1:
time: 856 us; the launch traced here: 855 us
  blocking collectives  418 us (49%)
  waiting for transfers between devices  347 us (41%)
  local copies, waits for them, and re-layouts  40.8 us (5%)
  matrix products  21.4 us (2%)
  between operations  15.1 us (2%)
  starting transfers between devices  11 us (1%)
    unnamed x2, waiting for transfers between devices  347 us
    psum x1, blocking collectives, local(): mixing_grad = lax.psum(lax.psum(local_mix, 'dp'), ('gx', 'gy')) * mix_scale  138 us
    all_gather x1, blocking collectives, local(): lax.all_gather(spectral_weight, ('gx', 'gy'), axis=0, tiled=True)  112 us
    psum x1, blocking collectives, local(): spectral_grad = lax.psum(share, 'dp') * spec_scale  67.2 us
    all_to_all x1, blocking collectives, to_cells(): lax.all_to_all(lax.all_to_all(plane_block, 'gx', split_axis=2, concat_axi...  31.7 us
    all_to_all x1, blocking collectives, to_cells(): lax.all_to_all(plane_block, 'gx', split_axis=2, concat_axis=1, tiled=True)  29 us
    all_to_all x1, blocking collectives, to_planes(): lax.all_to_all(lax.all_to_all(block, 'gx', split_axis=1, concat_axis=2, t...  25 us
  transfers between devices with their start and end apart: 3, of which 1 were waited for; matrix products, arithmetic and copies ran while one was open for 2% of the time, Pallas kernels for 0%

profile of v1, /device:TPU:8, one launch (start us, length us, event | category | flops | bytes accessed | tf_op | source)
XLA Modules:
  0.0 854.8 jit_solution(16476314305042747207)
XLA Ops:
  7.2 1.6 reshape_squeeze.3
  8.8 1.1 copy.251
  9.9 4.3 all-to-all-start
  14.2 112.5 %all_gather.3 = bf16[288,2,20,20]{3,1,2,0:T(2,128)(2,1)S(1)} all-gather(bf16[9,2,20,20]{3,1,2,0:T(2,128)(2,1)S(1)} %copy-done.5), channel_id=1, replica_groups=mesh['dp'=16,'gx'=8,'gy'=4] {'gx','gy'}, dimensions={0}, use_global_device_ids=true | all-gather | bytes 475200 | tf_op jit(solution)/shard_map/all_gather | solution.py:141
  126.7 1.3 copy.252
  127.9 0.3 copy.253
  128.3 0.9 copy.254
  129.2 6.7 all-to-all-start.1
  135.9 5.7 fusion.165
  141.6 6.4 copy.317
  148.0 4.7 copy.318
  152.6 1.2 copy.255
  153.8 0.3 copy.256
  154.1 0.6 fusion.9
  154.7 0.6 convolution_bitcast_fusion
  155.4 0.9 fusion.33
  156.3 0.9 fusion.29
  157.2 0.9 fusion.15
  158.2 0.9 fusion.14
  159.1 0.3 copy.262
  159.4 0.2 stack.24
  159.6 0.3 copy.259
  159.8 0.2 stack.23
  160.2 0.3 fusion.22
  160.7 0.2 copy.265
  160.9 0.4 fusion.41
  161.3 0.4 fusion.49
  161.8 0.2 copy.266
  162.0 0.4 fusion.12
  162.5 0.4 fusion.13
  162.9 2.2 fusion.24
  165.1 2.2 fusion.8
  167.3 1.3 copy.271
  168.7 29.0 %all_to_all.81 = f32[20,1,128,128]{3,1,0,2:T(1,128)S(1)} all-to-all(f32[20,1,128,128]{3,1,0,2:T(1,128)S(1)} %copy.271), channel_id=1, replica_groups=mesh['dp'=16,'gx'=8,'gy'=4] {'gx'}, dimensions={2} | all-to-all | bytes 2621440 | tf_op jit(solution)/shard_map/all_to_all | solution.py:119
  197.8 0.4 copy.273
  198.2 31.7 %all_to_all.82 = f32[20,8,16,128]{3,1,0,2:T(8,128)S(1)} all-to-all(f32[20,8,16,128]{3,1,0,2:T(8,128)S(1)} %copy.273), channel_id=1, replica_groups=mesh['dp'=16,'gx'=8,'gy'=4] {'gy'}, dimensions={2} | all-to-all | bytes 2621440 | tf_op jit(solution)/shard_map/all_to_all | solution.py:118
  229.9 0.8 copy.357
  230.8 0.5 reshape_reshape.3
  231.3 0.5 copy-done.4
  231.8 4.7 fusion.6
  236.6 0.3 reshape.261
  236.8 14.2 %all_to_all.83 = bf16[20,32,4,128]{3,2,0,1:T(4,128)(2,1)S(1)} all-to-all(bf16[20,32,4,128]{3,2,0,1:T(4,128)(2,1)S(1)} %reshape.261), channel_id=1, replica_groups=mesh['dp'=16,'gx'=8,'gy'=4] {'gx'}, dimensions={1} | all-to-all | bytes 1310720 | tf_op jit(solution)/shard_map/all_to_all | solution.py:101
  251.0 0.3 copy.281
  251.4 25.0 %all_to_all.84 = bf16[20,4,32,128]{3,2,0,1:T(8,128)(2,1)S(1)} all-to-all(bf16[20,4,32,128]{3,2,0,1:T(8,128)(2,1)S(1)} %copy.282), channel_id=1, replica_groups=mesh['dp'=16,'gx'=8,'gy'=4] {'gy'}, dimensions={1} | all-to-all | bytes 1310720 | tf_op jit(solution)/shard_map/all_to_all | solution.py:100
  276.4 0.3 copy.284
  276.7 0.6 fusion.59
  277.4 0.6 fusion.63
  278.0 0.9 fusion.27
  278.9 0.9 fusion.35
  279.9 0.9 fusion.11
  280.8 0.9 fusion.10
  281.7 0.3 copy.289
  282.0 0.2 stack.27
  282.2 0.3 copy.287
  283.1 6.0 copy.290
  289.1 1.3 dynamic-slice
  291.1 1.0 copy.292
  292.2 0.7 convolution_bitcast_fusion.1
  292.9 347.3 %all-reduce.4.cloned.1.call-done = f32[288,2,20,20]{3,1,2,0:T(2,128)} async-done(((f32[288,2,20,20]{3,1,2,0:T(2,128)}), f32[288,2,20,20]{3,1,2,0:T(2,128)}) %all-reduce.4.cloned.1.call-update) | async-done | bytes 921616
  640.1 0.9 constant_dynamic-slice_fusion
  641.1 67.2 %all-reduce.1 = (f32[9,2,20,20]{3,1,2,0:T(2,128)S(1)}, f32[20,20]{0,1:T(8,128)S(1)}) all-reduce(f32[9,2,20,20]{3,1,2,0:T(2,128)S(1)} %constant_dynamic-slice_fusion, f32[20,20]{0,1:T(8,128)S(1)} %convolution_bitcast_fusion.1), channel_id=1, replica_groups=mesh['dp'=16,'gx'=8,'gy'=4] {'dp'}, use_global_device_ids=true, to_apply=%region_1.2 | all-reduce | flops 7600 | bytes 60800 | tf_op jit(solution)/shard_map/psum | solution.py:154
  708.3 0.8 broadcast_multiply_fusion
  709.1 138.2 %psum.23 = f32[20,20]{0,1:T(8,128)S(1)} all-reduce(f32[20,20]{0,1:T(8,128)S(1)} %get-tuple-element.34), channel_id=1, replica_groups=mesh['dp'=16,'gx'=8,'gy'=4] {'gx','gy'}, use_global_device_ids=true, to_apply=%region_3.4 | all-reduce | flops 400 | bytes 3200 | tf_op jit(solution)/shard_map/psum | solution.py:155
  847.2 0.7 copy.293
  (34 shorter events, 1.3 us)
Async XLA Ops:
  7.2 224.1 %copy-start = (bf16[20,20]{1,0:T(8,128)(2,1)S(1)}, bf16[20,20]{1,0:T(8,128)(2,1)}, u32[]{:S(2)}) copy-start(bf16[20,20]{1,0:T(8,128)(2,1)} %param.6) | copy-start | bytes 2404
  8.8 5.4 copy-start.5
  9.9 116.8 %all-to-all-start = ((bf16[20,32,4,128]{3,2,0,1:T(4,128)(2,1)}), bf16[20,32,4,128]{3,2,0,1:T(4,128)(2,1)}, u32[]{:S(2)}, u32[]{:S(2)}) async-start(bf16[20,32,4,128]{3,2,0,1:T(4,128)(2,1)} %copy.251), calls=%async_computation | async-start | bytes 1310720 | tf_op jit(solution)/shard_map/all_to_all | solution.py:101
  129.2 23.5 %all-to-all-start.1 = ((bf16[20,4,32,128]{3,2,0,1:T(8,128)(2,1)}), bf16[20,4,32,128]{3,2,0,1:T(8,128)(2,1)}, u32[]{:S(2)}, u32[]{:S(2)}) async-start(bf16[20,4,32,128]{3,2,0,1:T(8,128)(2,1)} %copy.254), calls=%async_computation.1 | async-start | bytes 1310720 | tf_op jit(solution)/shard_map/all_to_all | solution.py:100
  135.9 504.2 %all-reduce.4.cloned.1.call-start = ((), (), s32[]{:S(2)}) async-start(), calls=%async_computation.6 | async-start | bytes 11796480
  141.6 6.4 copy-start.1
  155.4 4.8 copy-start.2
  230.8 1.1 copy-start.4
  289.1 2.0 copy-start.3
Sparse Core Ops, SparseCore 0:
  289.3 350.8 all-reduce.3
